TPU v7x, 128 devices: a whole 4x4x4 slice. The times are simulated.
128 devices in a mesh: sweep: 8 (over y, core), leaf: 16 (over x, z).
Axes of the slice: x: 4, y: 4, z: 4, core: 2. Of those that a mesh axis runs over, the one named last changes fastest.
Arguments:
- rhs_interior: float32 [8, 16, 2, 4, 1024], P('sweep', 'leaf'), may hold values from -6 to 6
- rhs_separator: float32 [8, 2, 4, 2560], P('sweep', None, None, 'leaf'), may hold values from -6 to 6
- leaf_inverse: bfloat16 [8, 16, 2, 1024, 1024], P('sweep', 'leaf'), may hold values from -1.2 to 1.2
- leaf_to_front: bfloat16 [8, 16, 2, 256, 2560], P('sweep', 'leaf'), may hold values from -0.09375 to 0.09375
- front_to_leaf: bfloat16 [8, 16, 2, 2560, 256], P('sweep', 'leaf'), may hold values from -0.0390625 to 0.0390625
- front_inverse: bfloat16 [8, 2, 2560, 2560], P('sweep', None, None, 'leaf'), may hold values from -1.2 to 1.2
- front_sizes: int32 [8, 16], P('sweep', 'leaf'), may hold values from 1 to 768, 9216 in all within a row
Outputs:
- sol_interior: float32 [8, 16, 2, 4, 1024], P('sweep', 'leaf')
- sol_separator: float32 [8, 2, 4, 2560], P('sweep', None, None, 'leaf')
Inputs may be any that keep to these rules, and one draw needn't show every extreme that they name: `front_sizes`: in each panel the values sum to 9216 and one of them equals 768.
All inputs are finite; a program needn't handle non-finite values. No bound on the sum of `front_sizes` on one device may be relied on, other than what follows from the above.
Results may differ from a plain program's by a relative error of at most 0.038.
Values may be sent and summed in bfloat16 or wider, within the bound.
A program may use at most 128 MiB of HBM per device.

v0:
```python
import jax
import jax.numpy as jnp
from jax import lax
from jax.sharding import PartitionSpec as P

PORT_CELLS = 256
PLANES = 4


coupling = 1.0


def shifted(shard, axis, by):
    devices = lax.axis_size(axis)
    pairs = [(i, i + by) for i in range(devices) if 0 <= i + by < devices]
    return lax.ppermute(shard, axis, pairs)


def cmul(vec, mat):
    rows = vec.reshape(-1, vec.shape[-1])
    part_re = jnp.dot(rows, mat[0], preferred_element_type=jnp.float32).reshape(2, -1, mat.shape[2])
    part_im = jnp.dot(rows, mat[1], preferred_element_type=jnp.float32).reshape(2, -1, mat.shape[2])
    return jnp.stack([part_re[0] - part_im[1], part_im[0] + part_re[1]])


def plane_of(values, plane):
    shaped = values.reshape(values.shape[:-1] + (values.shape[-1] // PLANES, PLANES))
    return shaped[..., plane]


def put_plane(values, plane):
    spread = jnp.repeat(values, PLANES, axis=-1)
    position = lax.broadcasted_iota(jnp.int32, spread.shape, spread.ndim - 1) % PLANES
    return jnp.where(position == plane, spread, jnp.zeros_like(spread))


def send_ahead(sol_int, sol_sep):
    leaf_width = sol_int.shape[-1] // PLANES
    joined = jnp.concatenate(
        [plane_of(sol_int, PLANES - 1), plane_of(sol_sep, PLANES - 1)], axis=-1
    )
    arrived = shifted(joined, "sweep", 1)
    return (put_plane(arrived[..., :leaf_width], 0), put_plane(arrived[..., leaf_width:], 0))


def send_behind(sol_int, sol_sep):
    leaf_width = sol_int.shape[-1] // PLANES
    joined = jnp.concatenate([plane_of(sol_int, 0), plane_of(sol_sep, 0)], axis=-1)
    arrived = shifted(joined, "sweep", -1)
    return (
        put_plane(arrived[..., :leaf_width], PLANES - 1),
        put_plane(arrived[..., leaf_width:], PLANES - 1),
    )


def body(
    rhs_interior,
    rhs_separator,
    leaf_inverse,
    leaf_to_front,
    front_to_leaf,
    front_inverse,
    front_sizes,
):
    rhs_int = rhs_interior[0, 0]
    rhs_sep = rhs_separator[0]
    inv_leaf = leaf_inverse[0, 0]
    to_front = leaf_to_front[0, 0]
    to_leaf = front_to_leaf[0, 0]
    inv_front = front_inverse[0]
    cell_count = rhs_int.shape[-1]
    live_mask = (
        lax.broadcasted_iota(jnp.int32, (cell_count,), 0) < PORT_CELLS + front_sizes[0, 0]
    ).astype(jnp.float32)

    def panel_solve(h_int, h_sep):
        inner = cmul((h_int * live_mask).astype(jnp.bfloat16), inv_leaf)
        leaf_term = cmul(inner[..., :PORT_CELLS].astype(jnp.bfloat16), to_front)
        front_rhs = h_sep - lax.psum_scatter(
            leaf_term.astype(jnp.bfloat16), "leaf", scatter_dimension=2, tiled=True
        ).astype(jnp.float32)
        front_low = front_rhs.astype(jnp.bfloat16)
        rows_of = inv_front
        front_sol = cmul(lax.all_gather(front_low, "leaf", axis=2, tiled=True), rows_of)
        rows_of = to_leaf
        port_corr = cmul(
            lax.all_gather(front_sol.astype(jnp.bfloat16), "leaf", axis=2, tiled=True), rows_of
        )
        leaf_sol = (
            inner - cmul(port_corr.astype(jnp.bfloat16), inv_leaf[:, :PORT_CELLS, :])
        ) * live_mask
        return (leaf_sol, front_sol)

    panels = lax.axis_size("sweep")
    fwd_int, fwd_sep = panel_solve(rhs_int, rhs_sep)
    for step in range(panels - 1):
        add_int, add_sep = send_ahead(fwd_int, fwd_sep)
        fwd_int, fwd_sep = panel_solve(rhs_int + coupling * add_int, rhs_sep + coupling * add_sep)
    sol_int, sol_sep = (fwd_int, fwd_sep)
    for step in range(panels - 1):
        back_int, back_sep = send_behind(sol_int, sol_sep)
        delta_int, delta_sep = panel_solve(coupling * back_int, coupling * back_sep)
        sol_int = fwd_int + delta_int
        sol_sep = fwd_sep + delta_sep
    return (sol_int[None, None], sol_sep[None])


def solution(mesh):
    placed = (
        P("sweep", "leaf", None, None, None),
        P("sweep", None, None, "leaf"),
        P("sweep", "leaf", None, None, None),
        P("sweep", "leaf", None, None, None),
        P("sweep", "leaf", None, None, None),
        P("sweep", None, None, "leaf"),
        P("sweep", "leaf"),
    )
    return jax.shard_map(
        body,
        mesh=mesh,
        in_specs=placed,
        out_specs=(P("sweep", "leaf", None, None, None), P("sweep", None, None, "leaf")),
        check_vma=False,
    )
```

profile of v0, /device:TPU:0, one launch (start us, length us, event | category | flops | bytes accessed | tf_op | source)
XLA Modules:
  0.0 2397.5 jit_solution(9624601254730239009)
XLA Ops:
  15.7 3.4 reshape.4285
  20.7 74.9 %reduce-scatter.46.cloned.1.call-done = bf16[160,8]{1,0:T(8,128)(2,1)} async-done(((bf16[2560,8]{1,0:T(8,128)(2,1)}), bf16[160,8]{1,0:T(8,128)(2,1)}) %reduce-scatter.46.cloned.1.call-update) | async-done | bytes 2576
  96.8 26.9 %all_gather.90 = bf16[2,4,2560]{1,0,2:T(2,128)(2,1)} all-gather(bf16[2,4,160]{1,0,2:T(2,128)(2,1)S(1)} %copy.188), channel_id=1, replica_groups=mesh['sweep'=8,'leaf'=16] {'leaf'}, dimensions={2}, use_global_device_ids=true | all-gather | bytes 43520 | tf_op jit(solution)/shard_map/all_gather | solution.py:84
  129.7 25.2 %all_gather.91 = bf16[2,4,2560]{1,0,2:T(2,128)(2,1)} all-gather(bf16[2,4,160]{1,0,2:T(2,128)(2,1)S(1)} %copy.190), channel_id=1, replica_groups=mesh['sweep'=8,'leaf'=16] {'leaf'}, dimensions={2}, use_global_device_ids=true | all-gather | bytes 43520 | tf_op jit(solution)/shard_map/all_gather | solution.py:87
  177.5 3.4 reshape.4287
  182.8 73.8 %reduce-scatter.48.cloned.1.call-done = bf16[160,8]{1,0:T(8,128)(2,1)} async-done(((bf16[2560,8]{1,0:T(8,128)(2,1)}), bf16[160,8]{1,0:T(8,128)(2,1)}) %reduce-scatter.48.cloned.1.call-update) | async-done | bytes 2576
  257.7 27.4 %all_gather.92 = bf16[2,4,2560]{1,0,2:T(2,128)(2,1)} all-gather(bf16[2,4,160]{1,0,2:T(2,128)(2,1)S(1)} %copy.198), channel_id=1, replica_groups=mesh['sweep'=8,'leaf'=16] {'leaf'}, dimensions={2}, use_global_device_ids=true | all-gather | bytes 43520 | tf_op jit(solution)/shard_map/all_gather | solution.py:84
  291.0 25.2 %all_gather.93 = bf16[2,4,2560]{1,0,2:T(2,128)(2,1)} all-gather(bf16[2,4,160]{1,0,2:T(2,128)(2,1)S(1)} %copy.200), channel_id=1, replica_groups=mesh['sweep'=8,'leaf'=16] {'leaf'}, dimensions={2}, use_global_device_ids=true | all-gather | bytes 43520 | tf_op jit(solution)/shard_map/all_gather | solution.py:87
  338.8 3.4 reshape.4289
  344.0 73.8 %reduce-scatter.50.cloned.1.call-done = bf16[160,8]{1,0:T(8,128)(2,1)} async-done(((bf16[2560,8]{1,0:T(8,128)(2,1)}), bf16[160,8]{1,0:T(8,128)(2,1)}) %reduce-scatter.50.cloned.1.call-update) | async-done | bytes 2576
  419.0 26.9 %all_gather.94 = bf16[2,4,2560]{1,0,2:T(2,128)(2,1)} all-gather(bf16[2,4,160]{1,0,2:T(2,128)(2,1)S(1)} %copy.208), channel_id=1, replica_groups=mesh['sweep'=8,'leaf'=16] {'leaf'}, dimensions={2}, use_global_device_ids=true | all-gather | bytes 43520 | tf_op jit(solution)/shard_map/all_gather | solution.py:84
  451.8 25.2 %all_gather.95 = bf16[2,4,2560]{1,0,2:T(2,128)(2,1)} all-gather(bf16[2,4,160]{1,0,2:T(2,128)(2,1)S(1)} %copy.210), channel_id=1, replica_groups=mesh['sweep'=8,'leaf'=16] {'leaf'}, dimensions={2}, use_global_device_ids=true | all-gather | bytes 43520 | tf_op jit(solution)/shard_map/all_gather | solution.py:87
  504.9 73.8 %reduce-scatter.52.cloned.1.call-done = bf16[160,8]{1,0:T(8,128)(2,1)} async-done(((bf16[2560,8]{1,0:T(8,128)(2,1)}), bf16[160,8]{1,0:T(8,128)(2,1)}) %reduce-scatter.52.cloned.1.call-update) | async-done | bytes 2576
  579.9 26.9 %all_gather.96 = bf16[2,4,2560]{1,0,2:T(2,128)(2,1)} all-gather(bf16[2,4,160]{1,0,2:T(2,128)(2,1)S(1)} %copy.218), channel_id=1, replica_groups=mesh['sweep'=8,'leaf'=16] {'leaf'}, dimensions={2}, use_global_device_ids=true | all-gather | bytes 43520 | tf_op jit(solution)/shard_map/all_gather | solution.py:84
  612.7 25.2 %all_gather.97 = bf16[2,4,2560]{1,0,2:T(2,128)(2,1)} all-gather(bf16[2,4,160]{1,0,2:T(2,128)(2,1)S(1)} %copy.220), channel_id=1, replica_groups=mesh['sweep'=8,'leaf'=16] {'leaf'}, dimensions={2}, use_global_device_ids=true | all-gather | bytes 43520 | tf_op jit(solution)/shard_map/all_gather | solution.py:87
  666.0 73.6 %reduce-scatter.54.cloned.1.call-done = bf16[160,8]{1,0:T(8,128)(2,1)} async-done(((bf16[2560,8]{1,0:T(8,128)(2,1)}), bf16[160,8]{1,0:T(8,128)(2,1)}) %reduce-scatter.54.cloned.1.call-update) | async-done | bytes 2576
  740.7 27.0 %all_gather.98 = bf16[2,4,2560]{1,0,2:T(2,128)(2,1)} all-gather(bf16[2,4,160]{1,0,2:T(2,128)(2,1)S(1)} %copy.228), channel_id=1, replica_groups=mesh['sweep'=8,'leaf'=16] {'leaf'}, dimensions={2}, use_global_device_ids=true | all-gather | bytes 43520 | tf_op jit(solution)/shard_map/all_gather | solution.py:84
  773.6 25.2 %all_gather.99 = bf16[2,4,2560]{1,0,2:T(2,128)(2,1)} all-gather(bf16[2,4,160]{1,0,2:T(2,128)(2,1)S(1)} %copy.230), channel_id=1, replica_groups=mesh['sweep'=8,'leaf'=16] {'leaf'}, dimensions={2}, use_global_device_ids=true | all-gather | bytes 43520 | tf_op jit(solution)/shard_map/all_gather | solution.py:87
  826.6 73.7 %reduce-scatter.56.cloned.1.call-done = bf16[160,8]{1,0:T(8,128)(2,1)} async-done(((bf16[2560,8]{1,0:T(8,128)(2,1)}), bf16[160,8]{1,0:T(8,128)(2,1)}) %reduce-scatter.56.cloned.1.call-update) | async-done | bytes 2576
  901.5 26.9 %all_gather.100 = bf16[2,4,2560]{1,0,2:T(2,128)(2,1)} all-gather(bf16[2,4,160]{1,0,2:T(2,128)(2,1)S(1)} %copy.238), channel_id=1, replica_groups=mesh['sweep'=8,'leaf'=16] {'leaf'}, dimensions={2}, use_global_device_ids=true | all-gather | bytes 43520 | tf_op jit(solution)/shard_map/all_gather | solution.py:84
  934.3 25.2 %all_gather.101 = bf16[2,4,2560]{1,0,2:T(2,128)(2,1)} all-gather(bf16[2,4,160]{1,0,2:T(2,128)(2,1)S(1)} %copy.240), channel_id=1, replica_groups=mesh['sweep'=8,'leaf'=16] {'leaf'}, dimensions={2}, use_global_device_ids=true | all-gather | bytes 43520 | tf_op jit(solution)/shard_map/all_gather | solution.py:87
  987.3 73.8 %reduce-scatter.58.cloned.1.call-done = bf16[160,8]{1,0:T(8,128)(2,1)} async-done(((bf16[2560,8]{1,0:T(8,128)(2,1)}), bf16[160,8]{1,0:T(8,128)(2,1)}) %reduce-scatter.58.cloned.1.call-update) | async-done | bytes 2576
  1062.4 26.9 %all_gather.102 = bf16[2,4,2560]{1,0,2:T(2,128)(2,1)} all-gather(bf16[2,4,160]{1,0,2:T(2,128)(2,1)S(1)} %copy.248), channel_id=1, replica_groups=mesh['sweep'=8,'leaf'=16] {'leaf'}, dimensions={2}, use_global_device_ids=true | all-gather | bytes 43520 | tf_op jit(solution)/shard_map/all_gather | solution.py:84
  1095.2 25.2 %all_gather.103 = bf16[2,4,2560]{1,0,2:T(2,128)(2,1)} all-gather(bf16[2,4,160]{1,0,2:T(2,128)(2,1)S(1)} %copy.250), channel_id=1, replica_groups=mesh['sweep'=8,'leaf'=16] {'leaf'}, dimensions={2}, use_global_device_ids=true | all-gather | bytes 43520 | tf_op jit(solution)/shard_map/all_gather | solution.py:87
  1148.5 73.6 %reduce-scatter.60.cloned.1.call-done = bf16[160,8]{1,0:T(8,128)(2,1)} async-done(((bf16[2560,8]{1,0:T(8,128)(2,1)}), bf16[160,8]{1,0:T(8,128)(2,1)}) %reduce-scatter.60.cloned.1.call-update) | async-done | bytes 2576
  1223.2 26.9 %all_gather.104 = bf16[2,4,2560]{1,0,2:T(2,128)(2,1)} all-gather(bf16[2,4,160]{1,0,2:T(2,128)(2,1)S(1)} %copy.256), channel_id=1, replica_groups=mesh['sweep'=8,'leaf'=16] {'leaf'}, dimensions={2}, use_global_device_ids=true | all-gather | bytes 43520 | tf_op jit(solution)/shard_map/all_gather | solution.py:84
  1256.1 25.3 %all_gather.105 = bf16[2,4,2560]{1,0,2:T(2,128)(2,1)} all-gather(bf16[2,4,160]{1,0,2:T(2,128)(2,1)S(1)} %copy.258), channel_id=1, replica_groups=mesh['sweep'=8,'leaf'=16] {'leaf'}, dimensions={2}, use_global_device_ids=true | all-gather | bytes 43520 | tf_op jit(solution)/shard_map/all_gather | solution.py:87
  1308.1 72.1 %reduce-scatter.62.cloned.1.call-done = bf16[160,8]{1,0:T(8,128)(2,1)} async-done(((bf16[2560,8]{1,0:T(8,128)(2,1)}), bf16[160,8]{1,0:T(8,128)(2,1)}) %reduce-scatter.62.cloned.1.call-update) | async-done | bytes 2576
  1381.3 27.0 %all_gather.106 = bf16[2,4,2560]{1,0,2:T(2,128)(2,1)} all-gather(bf16[2,4,160]{1,0,2:T(2,128)(2,1)S(1)} %copy.269), channel_id=1, replica_groups=mesh['sweep'=8,'leaf'=16] {'leaf'}, dimensions={2}, use_global_device_ids=true | all-gather | bytes 43520 | tf_op jit(solution)/shard_map/all_gather | solution.py:84
  1414.2 25.1 %all_gather.107 = bf16[2,4,2560]{1,0,2:T(2,128)(2,1)} all-gather(bf16[2,4,160]{1,0,2:T(2,128)(2,1)S(1)} %copy.271), channel_id=1, replica_groups=mesh['sweep'=8,'leaf'=16] {'leaf'}, dimensions={2}, use_global_device_ids=true | all-gather | bytes 43520 | tf_op jit(solution)/shard_map/all_gather | solution.py:87
  1466.3 72.1 %reduce-scatter.64.cloned.1.call-done = bf16[160,8]{1,0:T(8,128)(2,1)} async-done(((bf16[2560,8]{1,0:T(8,128)(2,1)}), bf16[160,8]{1,0:T(8,128)(2,1)}) %reduce-scatter.64.cloned.1.call-update) | async-done | bytes 2576
  1539.6 26.9 %all_gather.108 = bf16[2,4,2560]{1,0,2:T(2,128)(2,1)} all-gather(bf16[2,4,160]{1,0,2:T(2,128)(2,1)S(1)} %copy.280), channel_id=1, replica_groups=mesh['sweep'=8,'leaf'=16] {'leaf'}, dimensions={2}, use_global_device_ids=true | all-gather | bytes 43520 | tf_op jit(solution)/shard_map/all_gather | solution.py:84
  1572.4 25.2 %all_gather.109 = bf16[2,4,2560]{1,0,2:T(2,128)(2,1)} all-gather(bf16[2,4,160]{1,0,2:T(2,128)(2,1)S(1)} %copy.282), channel_id=1, replica_groups=mesh['sweep'=8,'leaf'=16] {'leaf'}, dimensions={2}, use_global_device_ids=true | all-gather | bytes 43520 | tf_op jit(solution)/shard_map/all_gather | solution.py:87
  1624.8 71.6 %reduce-scatter.66.cloned.1.call-done = bf16[160,8]{1,0:T(8,128)(2,1)} async-done(((bf16[2560,8]{1,0:T(8,128)(2,1)}), bf16[160,8]{1,0:T(8,128)(2,1)}) %reduce-scatter.66.cloned.1.call-update) | async-done | bytes 2576
  1697.6 26.9 %all_gather.110 = bf16[2,4,2560]{1,0,2:T(2,128)(2,1)} all-gather(bf16[2,4,160]{1,0,2:T(2,128)(2,1)S(1)} %copy.291), channel_id=1, replica_groups=mesh['sweep'=8,'leaf'=16] {'leaf'}, dimensions={2}, use_global_device_ids=true | all-gather | bytes 43520 | tf_op jit(solution)/shard_map/all_gather | solution.py:84
  1730.4 25.2 %all_gather.111 = bf16[2,4,2560]{1,0,2:T(2,128)(2,1)} all-gather(bf16[2,4,160]{1,0,2:T(2,128)(2,1)S(1)} %copy.293), channel_id=1, replica_groups=mesh['sweep'=8,'leaf'=16] {'leaf'}, dimensions={2}, use_global_device_ids=true | all-gather | bytes 43520 | tf_op jit(solution)/shard_map/all_gather | solution.py:87
  1782.4 72.0 %reduce-scatter.68.cloned.1.call-done = bf16[160,8]{1,0:T(8,128)(2,1)} async-done(((bf16[2560,8]{1,0:T(8,128)(2,1)}), bf16[160,8]{1,0:T(8,128)(2,1)}) %reduce-scatter.68.cloned.1.call-update) | async-done | bytes 2576
  1855.6 27.0 %all_gather.112 = bf16[2,4,2560]{1,0,2:T(2,128)(2,1)} all-gather(bf16[2,4,160]{1,0,2:T(2,128)(2,1)S(1)} %copy.302), channel_id=1, replica_groups=mesh['sweep'=8,'leaf'=16] {'leaf'}, dimensions={2}, use_global_device_ids=true | all-gather | bytes 43520 | tf_op jit(solution)/shard_map/all_gather | solution.py:84
  1888.4 25.2 %all_gather.113 = bf16[2,4,2560]{1,0,2:T(2,128)(2,1)} all-gather(bf16[2,4,160]{1,0,2:T(2,128)(2,1)S(1)} %copy.304), channel_id=1, replica_groups=mesh['sweep'=8,'leaf'=16] {'leaf'}, dimensions={2}, use_global_device_ids=true | all-gather | bytes 43520 | tf_op jit(solution)/shard_map/all_gather | solution.py:87
  1940.4 72.1 %reduce-scatter.70.cloned.1.call-done = bf16[160,8]{1,0:T(8,128)(2,1)} async-done(((bf16[2560,8]{1,0:T(8,128)(2,1)}), bf16[160,8]{1,0:T(8,128)(2,1)}) %reduce-scatter.70.cloned.1.call-update) | async-done | bytes 2576
  2013.6 26.9 %all_gather.114 = bf16[2,4,2560]{1,0,2:T(2,128)(2,1)} all-gather(bf16[2,4,160]{1,0,2:T(2,128)(2,1)S(1)} %copy.313), channel_id=1, replica_groups=mesh['sweep'=8,'leaf'=16] {'leaf'}, dimensions={2}, use_global_device_ids=true | all-gather | bytes 43520 | tf_op jit(solution)/shard_map/all_gather | solution.py:84
  2046.4 25.2 %all_gather.115 = bf16[2,4,2560]{1,0,2:T(2,128)(2,1)} all-gather(bf16[2,4,160]{1,0,2:T(2,128)(2,1)S(1)} %copy.315), channel_id=1, replica_groups=mesh['sweep'=8,'leaf'=16] {'leaf'}, dimensions={2}, use_global_device_ids=true | all-gather | bytes 43520 | tf_op jit(solution)/shard_map/all_gather | solution.py:87
  2098.6 71.9 %reduce-scatter.72.cloned.1.call-done = bf16[160,8]{1,0:T(8,128)(2,1)} async-done(((bf16[2560,8]{1,0:T(8,128)(2,1)}), bf16[160,8]{1,0:T(8,128)(2,1)}) %reduce-scatter.72.cloned.1.call-update) | async-done | bytes 2576
  2171.7 26.9 %all_gather.116 = bf16[2,4,2560]{1,0,2:T(2,128)(2,1)} all-gather(bf16[2,4,160]{1,0,2:T(2,128)(2,1)S(1)} %copy.324), channel_id=1, replica_groups=mesh['sweep'=8,'leaf'=16] {'leaf'}, dimensions={2}, use_global_device_ids=true | all-gather | bytes 43520 | tf_op jit(solution)/shard_map/all_gather | solution.py:84
  2204.5 25.2 %all_gather.117 = bf16[2,4,2560]{1,0,2:T(2,128)(2,1)} all-gather(bf16[2,4,160]{1,0,2:T(2,128)(2,1)S(1)} %copy.326), channel_id=1, replica_groups=mesh['sweep'=8,'leaf'=16] {'leaf'}, dimensions={2}, use_global_device_ids=true | all-gather | bytes 43520 | tf_op jit(solution)/shard_map/all_gather | solution.py:87
  2251.9 73.6 %reduce-scatter.74.cloned.1.call-done = bf16[160,8]{1,0:T(8,128)(2,1)} async-done(((bf16[2560,8]{1,0:T(8,128)(2,1)}), bf16[160,8]{1,0:T(8,128)(2,1)}) %reduce-scatter.74.cloned.1.call-update) | async-done | bytes 2576
  2326.6 26.9 %all_gather.118 = bf16[2,4,2560]{1,0,2:T(2,128)(2,1)} all-gather(bf16[2,4,160]{1,0,2:T(2,128)(2,1)S(1)} %copy.333), channel_id=1, replica_groups=mesh['sweep'=8,'leaf'=16] {'leaf'}, dimensions={2}, use_global_device_ids=true | all-gather | bytes 43520 | tf_op jit(solution)/shard_map/all_gather | solution.py:84
  2358.4 25.2 %all_gather.119 = bf16[2,4,2560]{1,0,2:T(2,128)(2,1)} all-gather(bf16[2,4,160]{1,0,2:T(2,128)(2,1)S(1)} %copy.335), channel_id=1, replica_groups=mesh['sweep'=8,'leaf'=16] {'leaf'}, dimensions={2}, use_global_device_ids=true | all-gather | bytes 43520 | tf_op jit(solution)/shard_map/all_gather | solution.py:87
  (887 shorter events, 490.2 us)
Async XLA Ops:
  7.2 88.5 %reduce-scatter.46.cloned.1.call-start = ((), (), s32[]{:S(2)}) async-start(), calls=%async_computation.15 | async-start | bytes 696320
  8.7 4.2 copy-start
  15.7 80.9 %copy-start.4 = (f32[1,2,4,160]{3,2,1,0:T(4,128)S(1)}, f32[1,2,4,160]{3,2,1,0:T(4,128)}, u32[]{:S(2)}) copy-start(f32[1,2,4,160]{3,2,1,0:T(4,128)} %param.8) | copy-start | bytes 15364
  19.2 237.4 %reduce-scatter.48.cloned.1.call-start = ((), (), s32[]{:S(2)}) async-start(), calls=%async_computation.16 | async-start | bytes 696320
  164.3 6.3 copy-start.3
  165.3 2.1 collective-permute-start
  181.0 236.8 %reduce-scatter.50.cloned.1.call-start = ((), (), s32[]{:S(2)}) async-start(), calls=%async_computation.17 | async-start | bytes 696320
  326.6 2.1 collective-permute-start.1
  342.3 236.4 %reduce-scatter.52.cloned.1.call-start = ((), (), s32[]{:S(2)}) async-start(), calls=%async_computation.18 | async-start | bytes 696320
  487.5 2.1 collective-permute-start.2
  503.1 236.4 %reduce-scatter.54.cloned.1.call-start = ((), (), s32[]{:S(2)}) async-start(), calls=%async_computation.19 | async-start | bytes 696320
  648.3 2.1 collective-permute-start.3
  664.0 236.3 %reduce-scatter.56.cloned.1.call-start = ((), (), s32[]{:S(2)}) async-start(), calls=%async_computation.20 | async-start | bytes 696320
  809.2 2.1 collective-permute-start.4
  824.8 236.4 %reduce-scatter.58.cloned.1.call-start = ((), (), s32[]{:S(2)}) async-start(), calls=%async_computation.21 | async-start | bytes 696320
  969.9 2.1 collective-permute-start.5
  985.6 236.5 %reduce-scatter.60.cloned.1.call-start = ((), (), s32[]{:S(2)}) async-start(), calls=%async_computation.22 | async-start | bytes 696320
  1130.9 2.1 collective-permute-start.6
  1146.5 233.6 %reduce-scatter.62.cloned.1.call-start = ((), (), s32[]{:S(2)}) async-start(), calls=%async_computation.23 | async-start | bytes 696320
  1291.8 3.1 collective-permute-start.7
  1306.3 232.1 %reduce-scatter.64.cloned.1.call-start = ((), (), s32[]{:S(2)}) async-start(), calls=%async_computation.24 | async-start | bytes 696320
  1449.8 3.3 collective-permute-start.8
  1464.5 231.9 %reduce-scatter.66.cloned.1.call-start = ((), (), s32[]{:S(2)}) async-start(), calls=%async_computation.25 | async-start | bytes 696320
  1608.1 3.1 collective-permute-start.9
  1622.6 231.7 %reduce-scatter.68.cloned.1.call-start = ((), (), s32[]{:S(2)}) async-start(), calls=%async_computation.26 | async-start | bytes 696320
  1766.1 3.1 collective-permute-start.10
  1780.6 231.8 %reduce-scatter.70.cloned.1.call-start = ((), (), s32[]{:S(2)}) async-start(), calls=%async_computation.27 | async-start | bytes 696320
  1924.0 3.1 collective-permute-start.11
  1938.6 232.0 %reduce-scatter.72.cloned.1.call-start = ((), (), s32[]{:S(2)}) async-start(), calls=%async_computation.28 | async-start | bytes 696320
  2082.1 3.1 collective-permute-start.12
  2096.7 228.8 %reduce-scatter.74.cloned.1.call-start = ((), (), s32[]{:S(2)}) async-start(), calls=%async_computation.29 | async-start | bytes 696320
  2240.2 3.1 collective-permute-start.13
  2251.6 104.7 %copy-start.2 = (bf16[1,2,2560,160]{2,3,1,0:T(8,128)(2,1)S(1)}, bf16[1,2,2560,160]{2,3,1,0:T(8,128)(2,1)}, u32[]{:S(2)}) copy-start(bf16[1,2,2560,160]{2,3,1,0:T(8,128)(2,1)} %param.12) | copy-start | bytes 4915204
  2356.6 29.8 %copy-start.1 = (bf16[1,1,2,2560,256]{4,3,2,1,0:T(8,128)(2,1)S(1)}, bf16[1,1,2,2560,256]{4,3,2,1,0:T(8,128)(2,1)}, u32[]{:S(2)}) copy-start(bf16[1,1,2,2560,256]{4,3,2,1,0:T(8,128)(2,1)} %param.11) | copy-start | bytes 7864324
Sparse Core Ops, SparseCore 0:
  19.3 76.3 reduce-scatter.45
  181.1 75.3 reduce-scatter.47
  342.4 75.3 reduce-scatter.49
  503.2 75.4 reduce-scatter.51
  664.1 75.3 reduce-scatter.53
  824.9 75.3 reduce-scatter.55
  985.7 75.4 reduce-scatter.57
  1146.6 75.3 reduce-scatter.59
  1306.4 73.6 reduce-scatter.61
  1464.7 73.7 reduce-scatter.63
  1622.8 73.6 reduce-scatter.65
  1780.7 73.5 reduce-scatter.67
  1938.7 73.6 reduce-scatter.69
  2096.8 73.7 reduce-scatter.71
  2251.8 73.6 reduce-scatter.73
where the time goes:
time: 2410 us; the launch traced here: 2400 us
  waiting for transfers between devices  1110 us (46%)
  blocking collectives  782 us (32%)
  local copies, waits for them, and re-layouts  264 us (11%)
  matrix products  192 us (8%)
    unnamed x30, waiting for transfers between devices  1100 us
    all_gather x15, blocking collectives, panel_solve(): lax.all_gather(front_low, 'leaf', axis=2, tiled=True)  404 us
    all_gather x15, blocking collectives, panel_solve(): lax.all_gather(front_sol.astype(jnp.bfloat16), 'leaf', axis=2, tiled=True)  378 us
    dot_general x75, matrix products, cmul(): jnp.dot(rows, mat[0], preferred_element_type=jnp.float32)  97.1 us
    unnamed x84, local copies, waits for them, and re-layouts  96.3 us
    dot_general x75, matrix products, cmul(): jnp.dot(rows, mat[1], preferred_element_type=jnp.float32)  95.3 us
  transfers between devices with their start and end apart: 29, of which 29 were waited for; matrix products, arithmetic and copies ran while one was open for 1% of the time, Pallas kernels for 0%

commit v1 on v0

v1 whole, which is shorter than its diff:
```python
import functools

import jax
import jax.numpy as jnp
from jax import lax
from jax.experimental import pallas as pl
from jax.experimental.pallas import tpu as pltpu
from jax.sharding import PartitionSpec as P

MESH = pl.DeviceIdType.MESH
F32, BF16 = jnp.float32, jnp.bfloat16
PORT = 256
PLANES = 4
SIDE = 4
GROUP = SIDE * SIDE
LEAF = 1024
SEP = 2560
OWN = SEP // GROUP
BLK = SEP // SIDE
SRC = 4
WIDE = 512


def hops(rel):
    return sum(min(d, SIDE - d) for d in divmod(rel, SIDE))


NEAR = sorted(range(GROUP), key=hops)
FAR = sorted(range(GROUP), key=lambda rel: -hops(rel))


def dot(lhs, rhs):
    return jnp.dot(lhs, rhs, preferred_element_type=F32)


def turned(vec):
    row = lax.broadcasted_iota(jnp.int32, vec.shape, 0)
    return jnp.where(row < SRC, -1.0, 1.0) * pltpu.roll(vec, SRC, axis=0)


def cmul(vec, w_re, w_im):
    return dot(vec.astype(BF16), w_re) + dot(turned(vec).astype(BF16), w_im)


def kernel(
    rint_ref, rsep_ref, fs_ref, l_hbm, a_hbm, c_hbm, f_hbm,
    oint_ref, osep_ref,
    lv, av, cv, fp, f2d, sel, selt, aaf, aab, naf, nab, aaf_nb, aab_nb, lq,
    inner_s, innerb_s, w_s, corr_s, f1_s, f_s, e_s, pre_s, is_s,
    base_src, fwd_src, bwd_src, f1_src, f2_src, uf_src, ub_src,
    base_rcv, fwd_rcv, bwd_rcv, f1_rcv, f2_rcv, uf_rcv, ub_rcv,
    load_sem, fp_send, fp_recv, aa_send, aa_recv, u_send, u_recv,
    base_send, base_recv, fwd_send, fwd_recv, bwd_send, bwd_recv,
    f1_send, f1_recv, f2_send, f2_recv,
):
    p, k = lax.axis_index("sweep"), lax.axis_index("leaf")
    last = lax.axis_size("sweep") - 1
    x, z = k // SIDE, lax.rem(k, SIDE)

    def to(rel):
        dx, dz = divmod(rel, SIDE)
        return lax.rem(x + dx, SIDE) * SIDE + lax.rem(z + dz, SIDE)

    def origin(rel):
        dx, dz = divmod(rel, SIDE)
        return lax.rem(x + SIDE - dx, SIDE) * SIDE + lax.rem(z + SIDE - dz, SIDE)

    loads = [
        pltpu.make_async_copy(l_hbm.at[0, 0], lv, load_sem.at[0]),
        pltpu.make_async_copy(a_hbm.at[0, 0], av, load_sem.at[1]),
        pltpu.make_async_copy(c_hbm.at[0, 0], cv, load_sem.at[2]),
        pltpu.make_async_copy(
            f_hbm.at[0, :, pl.ds(pl.multiple_of(z * BLK, BLK), BLK), :], fp.at[z], load_sem.at[3]
        ),
    ]
    for load in loads:
        load.start()

    barrier = pltpu.get_barrier_semaphore()
    for rel in range(1, GROUP):
        pl.semaphore_signal(barrier, inc=1, device_id={"leaf": to(rel)}, device_id_type=MESH)

    @pl.when(p < last)
    def _():
        for leaf in range(GROUP):
            pl.semaphore_signal(
                barrier, inc=1, device_id={"sweep": p + 1, "leaf": leaf}, device_id_type=MESH
            )

    @pl.when(p > 0)
    def _():
        for leaf in range(GROUP):
            pl.semaphore_signal(
                barrier, inc=1, device_id={"sweep": p - 1, "leaf": leaf}, device_id_type=MESH
            )

    @pl.when((p > 0) & (p < last))
    def _():
        pl.semaphore_wait(barrier, 3 * GROUP - 1)

    @pl.when((p == 0) | (p == last))
    def _():
        pl.semaphore_wait(barrier, 2 * GROUP - 1)

    def piece(dz):
        there = lax.rem(z + dz, SIDE)
        return pltpu.make_async_remote_copy(
            f_hbm.at[0, :, pl.ds(pl.multiple_of(there * BLK, BLK), BLK), :],
            fp.at[z],
            fp_send.at[dz],
            fp_recv.at[dz],
            device_id={"leaf": x * SIDE + there},
            device_id_type=MESH,
        )

    def piece_in(dz):
        here = lax.rem(z + SIDE - dz, SIDE)
        return pltpu.make_async_remote_copy(
            f_hbm.at[0, :, pl.ds(0, BLK), :],
            fp.at[here],
            fp_send.at[dz],
            fp_recv.at[dz],
            device_id={"leaf": x * SIDE + here},
            device_id_type=MESH,
        )

    for dz in range(1, SIDE):
        piece(dz).start()

    def out_copy(src, dst, send, recv, rel, slot, step):
        there = {"leaf": to(rel)}
        if step:
            there["sweep"] = p + step
        return pltpu.make_async_remote_copy(
            src.at[slot], dst.at[k], send.at[rel], recv.at[rel], device_id=there, device_id_type=MESH
        )

    def in_copy(src, dst, send, recv, rel, step):
        there = {"leaf": origin(rel)}
        if step:
            there["sweep"] = p - step
        return pltpu.make_async_remote_copy(
            src.at[0], dst.at[origin(rel)], send.at[rel], recv.at[rel],
            device_id=there, device_id_type=MESH,
        )

    def term_sends(src, dst, send, recv, step):
        return [
            out_copy(src, dst, send, recv, rel, SIDE if rel == 0 else lax.rem(to(rel), SIDE), step)
            for rel in FAR
            if step or rel
        ]

    def f_sends(src, dst, send, recv):
        return [out_copy(src, dst, send, recv, rel, 0, 0) for rel in FAR if rel]

    base_out = term_sends(base_src, base_rcv, base_send, base_recv, 0)
    fwd_out = term_sends(fwd_src, fwd_rcv, fwd_send, fwd_recv, 1)
    bwd_out = term_sends(bwd_src, bwd_rcv, bwd_send, bwd_recv, -1)
    f1_out = f_sends(f1_src, f1_rcv, f1_send, f1_recv)
    f2_out = f_sends(f2_src, f2_rcv, f2_send, f2_recv)

    def neighbour(src, dst, send, recv, step):
        return pltpu.make_async_remote_copy(
            src, dst, send, recv, device_id={"sweep": p + step}, device_id_type=MESH
        )

    aaf_out = neighbour(aaf, aaf_nb, aa_send.at[0], aa_recv.at[0], -1)
    aab_out = neighbour(aab, aab_nb, aa_send.at[1], aa_recv.at[1], 1)
    uf_out = neighbour(uf_src, uf_rcv, u_send.at[0], u_recv.at[0], 1)
    ub_out = neighbour(ub_src, ub_rcv, u_send.at[1], u_recv.at[1], -1)

    size = fs_ref[0, 0] + PORT
    col = lax.broadcasted_iota(jnp.int32, (1, LEAF), 1)
    live = jnp.where(col < size, 1.0, 0.0).astype(F32)

    def rows_of(ref):
        return jnp.concatenate([ref[0], ref[1]], axis=0)

    loads[0].wait()
    inner_s[...] = cmul(rows_of(rint_ref[0, 0]) * live, lv[0], lv[1])
    loads[1].wait()
    own = rows_of(rsep_ref[0]).astype(BF16)
    for blk in range(SIDE):
        cols = slice(blk * BLK, (blk + 1) * BLK)
        place = jnp.where(
            lax.broadcasted_iota(jnp.int32, (OWN, BLK), 1) + blk * BLK
            == lax.broadcasted_iota(jnp.int32, (OWN, BLK), 0) + k * OWN,
            1.0,
            0.0,
        ).astype(BF16)
        term = cmul(inner_s[:, :PORT], av[0, :, cols], av[1, :, cols]) - dot(own, place)
        base_src[blk] = term.astype(BF16)
    base_rcv[k] = base_src[z]
    for copy in base_out:
        copy.start()

    for at, plane in ((0, 0), (1, PLANES - 1)):
        cell = lax.broadcasted_iota(jnp.int32, (LEAF, PORT), 0)
        hit = (cell == lax.broadcasted_iota(jnp.int32, (LEAF, PORT), 1) * PLANES + plane) & (cell < size)
        sel[at] = jnp.where(hit, 1.0, 0.0).astype(BF16)
        cell = lax.broadcasted_iota(jnp.int32, (PORT, LEAF), 1)
        hit = (cell == lax.broadcasted_iota(jnp.int32, (PORT, LEAF), 0) * PLANES + plane) & (cell < size)
        selt[at] = jnp.where(hit, 1.0, 0.0).astype(BF16)

    def product(left_re, left_im, right, out):
        @pl.loop(0, SEP // WIDE)
        def _(i):
            cols = pl.ds(pl.multiple_of(i * WIDE, WIDE), WIDE)
            re, im = right[0, :, cols], right[1, :, cols]
            out[0, :, cols] = (dot(left_re, re) - dot(left_im, im)).astype(BF16)
            out[1, :, cols] = (dot(left_re, im) + dot(left_im, re)).astype(BF16)

    def picked(at):
        return (
            dot(selt[at], lv[0, :, :PORT]).astype(BF16),
            dot(selt[at], lv[1, :, :PORT]).astype(BF16),
        )

    @pl.when(p > 0)
    def _():
        left = picked(0)
        product(left[0], left[1], av, aaf)
        aaf_out.start()

    @pl.when(p < last)
    def _():
        left = picked(1)
        product(left[0], left[1], av, aab)
        aab_out.start()

    for at in range(2):
        for part in range(2):
            lq[at, part] = dot(lv[part, :PORT, :], sel[at]).astype(BF16)

    loads[3].wait()
    for dz in range(1, SIDE):
        piece_in(dz).wait_recv()
    for part in range(2):
        total = None
        for owner in range(SIDE):
            place = jnp.where(
                lax.broadcasted_iota(jnp.int32, (OWN, BLK), 1)
                == lax.broadcasted_iota(jnp.int32, (OWN, BLK), 0) + owner * OWN,
                1.0,
                0.0,
            ).astype(BF16)
            moved = dot(fp[owner, part], place)
            total = moved if total is None else total + moved
        f2d[part] = total.astype(BF16)
    loads[2].wait()

    def summed(src, dst, send, recv, step, total):
        for rel in NEAR:
            if step or rel:
                in_copy(src, dst, send, recv, rel, step).wait_recv()
            total = total + dst[origin(rel)].astype(F32)
        return total

    def ask(total, src, dst, out):
        part = cmul(-total, f2d[0], f2d[1]).astype(BF16)
        src[0] = part
        for copy in out:
            copy.start()
        dst[k] = part

    def answer(src, dst, send, recv):
        for rel in NEAR[1:]:
            in_copy(src, dst, send, recv, rel, 0).wait_recv()
        blocks = []
        for blk in range(SIDE):
            total = dst[blk * SIDE].astype(F32)
            for row in range(1, SIDE):
                total = total + dst[blk * SIDE + row].astype(F32)
            blocks.append(total)
        full = jnp.concatenate(blocks, axis=1)
        corr_s[...] = cmul(full, cv[0], cv[1])
        return full

    def keep(ref, full):
        for blk in range(SIDE):
            ref[blk] = full[:, blk * BLK : (blk + 1) * BLK]

    def shifted(blk, plane):
        lane = lax.rem(lax.broadcasted_iota(jnp.int32, blk.shape, 1), PLANES)
        only = jnp.where(lane == plane, blk, 0.0)
        return pltpu.roll(only, (BLK - PLANES + 1) if plane else (PLANES - 1), axis=1)

    def pass_on(na, src, out, plane, full_ref):
        for blk in range(SIDE):
            cols = slice(blk * BLK, (blk + 1) * BLK)
            src[blk] = (pre_s[:, cols] - cmul(corr_s[...], na[0, :, cols], na[1, :, cols])).astype(BF16)
        src[SIDE] = (src[z].astype(F32) - shifted(full_ref[z], plane)).astype(BF16)
        for copy in out:
            copy.start()

    def edge(at, src, copy):
        src[...] = (is_s[...] - cmul(corr_s[...], lq[at, 0], lq[at, 1])).astype(BF16)
        copy.start()

    def prepare(at, inner, aa):
        is_s[...] = dot(inner.astype(BF16), sel[at])
        pre_s[...] = cmul(is_s[...], aa[0], aa[1])

    def corrected(inner):
        return (inner - cmul(corr_s[...], lv[0, :PORT, :], lv[1, :PORT, :])) * live

    @pl.when(p > 0)
    def _():
        total = summed(base_src, base_rcv, base_send, base_recv, 0, jnp.zeros((2 * SRC, BLK), F32))
        total = summed(fwd_src, fwd_rcv, fwd_send, fwd_recv, 1, total)
        ask(total, f1_src, f1_rcv, f1_out)
        neighbour(uf_src, uf_rcv, u_send.at[0], u_recv.at[0], -1).wait_recv()
        spread = dot(uf_rcv[...], selt[0])
        inner_s[...] = inner_s[...] + cmul(spread, lv[0], lv[1])

    @pl.when(p == 0)
    def _():
        total = summed(base_src, base_rcv, base_send, base_recv, 0, jnp.zeros((2 * SRC, BLK), F32))
        ask(total, f1_src, f1_rcv, f1_out)

    @pl.when(p < last)
    def _():
        neighbour(aaf, aaf_nb, aa_send.at[0], aa_recv.at[0], 1).wait_recv()
        product(lq[1, 0], lq[1, 1], aaf_nb, naf)
        prepare(1, inner_s[...], aaf_nb)

    @pl.when(p > 0)
    def _():
        neighbour(aab, aab_nb, aa_send.at[1], aa_recv.at[1], -1).wait_recv()

    @pl.when(p == last)
    def _():
        product(lq[0, 0], lq[0, 1], aab_nb, nab)
        prepare(0, inner_s[...], aab_nb)

    keep(f1_s, answer(f1_src, f1_rcv, f1_send, f1_recv))

    @pl.when(p < last)
    def _():
        pass_on(naf, fwd_src, fwd_out, PLANES - 1, f1_s)
        edge(1, uf_src, uf_out)

    @pl.when(p == last)
    def _():
        pass_on(nab, bwd_src, bwd_out, 0, f1_s)
        edge(0, ub_src, ub_out)

    w_s[...] = corrected(inner_s[...])

    @pl.when((p > 0) & (p < last))
    def _():
        product(lq[0, 0], lq[0, 1], aab_nb, nab)

    @pl.when(p < last)
    def _():
        total = summed(bwd_src, bwd_rcv, bwd_send, bwd_recv, -1, jnp.zeros((2 * SRC, BLK), F32))
        ask(total, f2_src, f2_rcv, f2_out)
        neighbour(ub_src, ub_rcv, u_send.at[1], u_recv.at[1], 1).wait_recv()
        spread = dot(ub_rcv[...], selt[1])
        innerb_s[...] = cmul(spread, lv[0], lv[1])

    @pl.when((p > 0) & (p < last))
    def _():
        prepare(0, w_s[...] + innerb_s[...], aab_nb)

    @pl.when(p < last)
    def _():
        keep(f_s, answer(f2_src, f2_rcv, f2_send, f2_recv))
        for blk in range(SIDE):
            f1_s[blk] = f1_s[blk] + f_s[blk]

    @pl.when((p > 0) & (p < last))
    def _():
        pass_on(nab, bwd_src, bwd_out, 0, f1_s)
        edge(0, ub_src, ub_out)

    @pl.when(p < last)
    def _():
        w_s[...] = w_s[...] + corrected(innerb_s[...])

    oint_ref[0, 0, 0] = w_s[:SRC, :]
    oint_ref[0, 0, 1] = w_s[SRC:, :]
    block = f1_s[x]
    mine = jnp.zeros((2 * SRC, OWN), F32)
    for owner in range(SIDE):
        mine = jnp.where(z == owner, block[:, owner * OWN : (owner + 1) * OWN], mine)
    osep_ref[0, 0] = mine[:SRC]
    osep_ref[0, 1] = mine[SRC:]

    for dz in range(1, SIDE):
        piece(dz).wait_send()
    for copy in base_out + f1_out:
        copy.wait_send()

    @pl.when(p < last)
    def _():
        aab_out.wait_send()
        uf_out.wait_send()
        for copy in fwd_out + f2_out:
            copy.wait_send()

    @pl.when(p > 0)
    def _():
        aaf_out.wait_send()
        ub_out.wait_send()
        for copy in bwd_out:
            copy.wait_send()


def body(rhs_int, rhs_sep, leaf_inv, to_front, to_leaf, front_inv, sizes):
    vmem, anywhere = pl.BlockSpec(memory_space=pltpu.VMEM), pl.BlockSpec(memory_space=pl.ANY)
    rows = 2 * SRC

    def messages(count, width):
        return pltpu.VMEM((count, rows, width), BF16)

    scratch = [
        pltpu.VMEM((2, LEAF, LEAF), BF16),
        pltpu.VMEM((2, PORT, SEP), BF16),
        pltpu.VMEM((2, SEP, PORT), BF16),
        pltpu.VMEM((SIDE, 2, BLK, OWN), BF16),
        pltpu.VMEM((2, BLK, BLK), BF16),
        pltpu.VMEM((2, LEAF, PORT), BF16),
        pltpu.VMEM((2, PORT, LEAF), BF16),
    ]
    scratch += [pltpu.VMEM((2, PORT, SEP), BF16)] * 6
    scratch += [
        pltpu.VMEM((2, 2, PORT, PORT), BF16),
        pltpu.VMEM((rows, LEAF), F32),
        pltpu.VMEM((rows, LEAF), F32),
        pltpu.VMEM((rows, LEAF), F32),
        pltpu.VMEM((rows, PORT), F32),
        pltpu.VMEM((SIDE, rows, BLK), F32),
        pltpu.VMEM((SIDE, rows, BLK), F32),
        pltpu.VMEM((SIDE, rows, BLK), F32),
        pltpu.VMEM((rows, SEP), F32),
        pltpu.VMEM((rows, PORT), F32),
    ]
    scratch += [messages(SIDE + 1, BLK)] * 3 + [messages(1, BLK)] * 2
    scratch += [pltpu.VMEM((rows, PORT), BF16)] * 2
    scratch += [messages(GROUP, BLK)] * 5 + [pltpu.VMEM((rows, PORT), BF16)] * 2
    dma = pltpu.SemaphoreType.DMA
    scratch += [dma((4,)), dma((SIDE,)), dma((SIDE,))] + [dma((2,))] * 4 + [dma((GROUP,))] * 10
    return pl.pallas_call(
        kernel,
        out_shape=(
            jax.ShapeDtypeStruct(rhs_int.shape, F32),
            jax.ShapeDtypeStruct(rhs_sep.shape, F32),
        ),
        in_specs=[vmem, vmem, pl.BlockSpec(memory_space=pltpu.SMEM)] + [anywhere] * 4,
        out_specs=(vmem, vmem),
        scratch_shapes=scratch,
        compiler_params=pltpu.CompilerParams(
            collective_id=0, has_side_effects=True, vmem_limit_bytes=60 << 20
        ),
    )(rhs_int, rhs_sep, sizes, leaf_inv, to_front, to_leaf, front_inv)


def solution(mesh):
    placed = (
        P("sweep", "leaf", None, None, None),
        P("sweep", None, None, "leaf"),
        P("sweep", "leaf", None, None, None),
        P("sweep", "leaf", None, None, None),
        P("sweep", "leaf", None, None, None),
        P("sweep", None, None, "leaf"),
        P("sweep", "leaf"),
    )
    return jax.shard_map(
        body,
        mesh=mesh,
        in_specs=placed,
        out_specs=(P("sweep", "leaf", None, None, None), P("sweep", None, None, "leaf")),
        check_vma=False,
    )
```

time: 2410 us -> 204 us (0.08)
  waiting for transfers between devices: 1110 us -> 0 us
  blocking collectives: 782 us -> 0 us
  local copies, waits for them, and re-layouts: 264 us -> 6.67 us
  Pallas kernels: 0 us -> 195 us
  matrix products: 192 us -> 0 us
    unnamed x30 -> x0, waiting for transfers between devices: 1100 us -> none
    all_gather x30 -> x0, blocking collectives: 782 us -> none  [the longest x15 404 us: panel_solve(): lax.all_gather(front_low, 'leaf', axis=2, tiled=True)]
    pallas_call x0 -> x1, Pallas kernels: none -> 195 us  [body(): pl.pallas_call(kernel, out_shape=(jax.ShapeDtypeStruct(rhs_int.shape, F32...]
    dot_general x150 -> x0, matrix products: 192 us -> none  [the longest x75 97.1 us: cmul(): jnp.dot(rows, mat[0], preferred_element_type=jnp.float32)]
    unnamed x84 -> x3, local copies, waits for them, and re-layouts: 96.3 us -> 6.67 us
    all_gather x30 -> x0, local copies, waits for them, and re-layouts: 81.9 us -> none  [the longest x15 41 us: panel_solve(): lax.all_gather(front_sol.astype(jnp.bfloat16), 'leaf', axis=2, tiled=True)]
    another operation x151 -> x0, local copies, waits for them, and re-layouts: 45.6 us -> none  [cmul(): return jnp.stack([part_re[0] - part_im[1], part_im[0] + part_re[1]])]
  transfers between devices with their start and end apart: 29 -> 0, of which waited for: 29 -> 0; matrix products, arithmetic and copies ran while one was open for 1% -> 0% of each run, Pallas kernels for 0% -> 0%
where the time goes in v1:
time: 204 us; the launch traced here: 203 us
  Pallas kernels  195 us (96%)
  local copies, waits for them, and re-layouts  6.67 us (3%)
    pallas_call x1, Pallas kernels, body(): pl.pallas_call(kernel, out_shape=(jax.ShapeDtypeStruct(rhs_int.shape, F32...  195 us
    unnamed x3, local copies, waits for them, and re-layouts  6.67 us

profile of v1, /device:TPU:0, one launch (start us, length us, event | category | flops | bytes accessed | tf_op | source)
XLA Modules:
  0.0 203.3 jit_solution(16039381907340190755)
XLA Ops:
  1.3 4.0 %copy.9.f_hbm = bf16[1,2,2560,160]{3,2,1,0:T(8,128)(2,1)} copy(bf16[1,2,2560,160]{2,3,1,0:T(8,128)(2,1)} %param.12) | data formatting | bytes 3276800 | tf_op args[5]
  5.3 195.3 %shard_map.86 = (f32[1,1,2,4,1024]{4,3,2,1,0:T(4,128)}, f32[1,2,4,160]{3,2,1,0:T(4,128)}) custom-call(f32[1,1,2,4,1024]{4,3,2,1,0:T(4,128)} %rint_ref.1, f32[1,2,4,160]{3,2,1,0:T(4,128)} %rsep_ref.1, s32[1,1]{1,0:T(1,128)S(6)} %copy.12.fs_ref, bf16[1,1,2,1024,1024]{4,3,2,1,0:T(8,128)(2,1)} %l_hbm.1, bf16[1,1,2,256,2560]{4,3,2,1,0:T(8,128)(2,1)} %a_hbm.1, ...), custom_call_target="tpu_custom_call" | custom-call | tf_op jit(solution)/shard_map/pallas_call | solution.py:445
  200.6 1.4 copy.13
  202.0 1.3 copy.14

commit v2 on v1

v2 whole, which is shorter than its diff:
```python
import functools

import jax
import jax.numpy as jnp
from jax import lax
from jax.experimental import pallas as pl
from jax.experimental.pallas import tpu as pltpu
from jax.sharding import PartitionSpec as P

MESH = pl.DeviceIdType.MESH
F32, BF16 = jnp.float32, jnp.bfloat16
PORT = 256
PLANES = 4
SIDE = 4
GROUP = SIDE * SIDE
LEAF = 1024
SEP = 2560
OWN = SEP // GROUP
BLK = SEP // SIDE
SRC = 4
CALLER = 1
WIDE = 512


def hops(rel):
    return sum(min(d, SIDE - d) for d in divmod(rel, SIDE))


NEAR = sorted(range(GROUP), key=hops)
FAR = sorted(range(GROUP), key=lambda rel: -hops(rel))
AWAY = (2, 1, 3, 0)


def dot(lhs, rhs):
    return jnp.dot(lhs, rhs, preferred_element_type=F32)


def dot_t(lhs, rhs):
    return lax.dot_general(lhs, rhs, (((1,), (1,)), ((), ())), preferred_element_type=F32)


def turned(vec):
    row = lax.broadcasted_iota(jnp.int32, vec.shape, 0)
    return jnp.where(row < SRC, -1.0, 1.0) * pltpu.roll(vec, SRC, axis=0)


def cmul(vec, w_re, w_im):
    return dot(vec.astype(BF16), w_re) + dot(turned(vec).astype(BF16), w_im)


def kernel(
    rint_ref, rsep_ref, fs_ref, l_hbm, a_hbm, c_hbm, f_hbm,
    oint_ref, osep_ref,
    lv, av, cv, fo, f2t, f2d, place, sel, selt, aaf, aab, naf, nab, aaf_nb, aab_nb, lq,
    inner_s, innerb_s, w_s, corr_s, f1_s, pre_s, is_s,
    all_src, base_src, fwd_src, bwd_src, own_src, f1_src, f2_src, uf_src, ub_src,
    all_rcv, base_rcv, fwd_rcv, bwd_rcv, f1_rcv, f2_rcv, uf_rcv, ub_rcv,
    go_sem, turn_sem, load_sem, fp_send, fp_recv, aa_send, aa_recv, u_send, u_recv,
    base_send, base_recv, fwd_send, fwd_recv, bwd_send, bwd_recv,
    own_send, f1_send, f1_recv, f2_send, f2_recv,
):
    p, k = lax.axis_index("sweep"), lax.axis_index("leaf")
    last = lax.axis_size("sweep") - 1
    x, z = k // SIDE, lax.rem(k, SIDE)

    def to(rel):
        dx, dz = divmod(rel, SIDE)
        return lax.rem(x + dx, SIDE) * SIDE + lax.rem(z + dz, SIDE)

    def origin(rel):
        dx, dz = divmod(rel, SIDE)
        return lax.rem(x + SIDE - dx, SIDE) * SIDE + lax.rem(z + SIDE - dz, SIDE)

    def block_of(side):
        return pl.ds(pl.multiple_of(side * BLK, BLK), BLK)

    def owned_by(side):
        return pl.ds(pl.multiple_of(side * OWN, OWN), OWN)

    loads = [
        pltpu.make_async_copy(l_hbm.at[0, 0], lv, load_sem.at[0]),
        pltpu.make_async_copy(a_hbm.at[0, 0], av, load_sem.at[1]),
        pltpu.make_async_copy(c_hbm.at[0, 0], cv, load_sem.at[2]),
        pltpu.make_async_copy(
            f_hbm.at[0, :, :, block_of(z)], f2t.at[:, owned_by(z), :], load_sem.at[3]
        ),
    ]
    for load in loads:
        load.start()
    whole = pltpu.make_async_copy(f_hbm.at[0], fo, load_sem.at[4])

    @pl.when(p == 0)
    def _():
        whole.start()

    barrier = pltpu.get_barrier_semaphore()
    for rel in range(1, GROUP):
        pl.semaphore_signal(barrier, inc=1, device_id={"leaf": to(rel)}, device_id_type=MESH)

    @pl.when(p < last)
    def _():
        for leaf in range(GROUP):
            pl.semaphore_signal(
                barrier, inc=1, device_id={"sweep": p + 1, "leaf": leaf}, device_id_type=MESH
            )

    @pl.when(p > 0)
    def _():
        for leaf in range(GROUP):
            pl.semaphore_signal(
                barrier, inc=1, device_id={"sweep": p - 1, "leaf": leaf}, device_id_type=MESH
            )

    size = fs_ref[0, 0] + PORT
    for at, plane in ((0, 0), (1, PLANES - 1)):
        cell = lax.broadcasted_iota(jnp.int32, (LEAF, PORT), 0)
        hit = (cell == lax.broadcasted_iota(jnp.int32, (LEAF, PORT), 1) * PLANES + plane) & (cell < size)
        sel[at] = jnp.where(hit, 1.0, 0.0).astype(BF16)
        cell = lax.broadcasted_iota(jnp.int32, (PORT, LEAF), 1)
        hit = (cell == lax.broadcasted_iota(jnp.int32, (PORT, LEAF), 0) * PLANES + plane) & (cell < size)
        selt[at] = jnp.where(hit, 1.0, 0.0).astype(BF16)

    for blk in range(SIDE):
        hit = (
            lax.broadcasted_iota(jnp.int32, (OWN, BLK), 1) + blk * BLK
            == lax.broadcasted_iota(jnp.int32, (OWN, BLK), 0) + k * OWN
        )
        place[blk] = jnp.where(hit, 1.0, 0.0).astype(BF16)

    @pl.when((p > 0) & (p < last))
    def _():
        pl.semaphore_wait(barrier, 3 * GROUP - 1)

    @pl.when((p == 0) | (p == last))
    def _():
        pl.semaphore_wait(barrier, 2 * GROUP - 1)

    def piece(dz):
        there = lax.rem(z + dz, SIDE)
        return pltpu.make_async_remote_copy(
            f_hbm.at[0, :, :, block_of(there)],
            f2t.at[:, owned_by(z), :],
            fp_send.at[dz],
            fp_recv.at[dz],
            device_id={"leaf": x * SIDE + there},
            device_id_type=MESH,
        )

    def piece_in(dz):
        here = lax.rem(z + SIDE - dz, SIDE)
        return pltpu.make_async_remote_copy(
            f_hbm.at[0, :, :, block_of(z)],
            f2t.at[:, owned_by(here), :],
            fp_send.at[dz],
            fp_recv.at[dz],
            device_id={"leaf": x * SIDE + here},
            device_id_type=MESH,
        )

    first = lax.rem(p, 2) == 1

    @pl.when(first)
    def _():
        for dz in (1, SIDE - 1):
            piece(dz).start()

    def let_go():
        pl.semaphore_signal(go_sem, inc=1, device_id={"sweep": p + 1}, device_id_type=MESH)

    @pl.when(jnp.logical_not(first) & (p > 0))
    def _():
        let_go()

    def out_copy(src, dst, send, recv, rel, slot, step):
        there = {"leaf": to(rel)}
        if step:
            there["sweep"] = p + step
        return pltpu.make_async_remote_copy(
            src.at[slot], dst.at[k], send.at[rel], recv.at[rel], device_id=there, device_id_type=MESH
        )

    def in_copy(src, dst, send, recv, rel, step):
        there = {"leaf": origin(rel)}
        if step:
            there["sweep"] = p - step
        return pltpu.make_async_remote_copy(
            src.at[0], dst.at[origin(rel)], send.at[rel], recv.at[rel],
            device_id=there, device_id_type=MESH,
        )

    def term_sends(src, dst, send, recv, step):
        return {
            dz: [
                out_copy(
                    src, dst, send, recv, dx * SIDE + dz,
                    SIDE if dx == dz == 0 else lax.rem(z + dz, SIDE), step,
                )
                for dx in AWAY
                if step or dx or dz
            ]
            for dz in AWAY
        }

    def f_sends(src, dst, send, recv):
        return [out_copy(src, dst, send, recv, rel, 0, 0) for rel in FAR if rel]

    narrow = f1_src.at[:, :, :PORT], f1_rcv.at[:, :, :PORT]

    base_out = term_sends(base_src, base_rcv, base_send, base_recv, 0)
    all_out = f_sends(all_src, all_rcv, base_send, base_recv)
    own_out = term_sends(own_src, fwd_rcv, own_send, fwd_recv, 0)
    f0_out = f_sends(*narrow, f1_send, f1_recv)
    fwd_out = term_sends(fwd_src, fwd_rcv, fwd_send, fwd_recv, 1)
    bwd_out = term_sends(bwd_src, bwd_rcv, bwd_send, bwd_recv, -1)
    f1_out = f_sends(f1_src, f1_rcv, f1_send, f1_recv)
    f2_out = f_sends(f2_src, f2_rcv, f2_send, f2_recv)

    def flat(sends):
        return [copy for dz in AWAY for copy in sends[dz]]

    def neighbour(src, dst, send, recv, step):
        return pltpu.make_async_remote_copy(
            src, dst, send, recv, device_id={"sweep": p + step}, device_id_type=MESH
        )

    aaf_out = neighbour(aaf, aaf_nb, aa_send.at[0], aa_recv.at[0], -1)
    aab_out = neighbour(aab, aab_nb, aa_send.at[1], aa_recv.at[1], 1)
    uf_out = neighbour(uf_src, uf_rcv, u_send.at[0], u_recv.at[0], 1)
    ub_out = neighbour(ub_src, ub_rcv, u_send.at[1], u_recv.at[1], -1)

    col = lax.broadcasted_iota(jnp.int32, (1, LEAF), 1)
    live = jnp.where(col < size, 1.0, 0.0).astype(F32)

    def rows_of(ref):
        return jnp.concatenate([ref[0], ref[1]], axis=0)

    loads[0].wait()
    inner_s[...] = cmul(rows_of(rint_ref[0, 0]) * live, lv[0], lv[1])
    loads[1].wait()
    own = rows_of(rsep_ref[0]).astype(BF16)
    for blk in range(SIDE):
        cols = slice(blk * BLK, (blk + 1) * BLK)
        term = cmul(inner_s[:, :PORT], av[0, :, cols], av[1, :, cols]) - dot(own, place[blk])
        base_src[blk] = term.astype(BF16)
        all_src[0, :, cols] = term.astype(BF16)

    @pl.when(p == 0)
    def _():
        for copy in all_out:
            copy.start()

    @pl.when(p > 0)
    def _():
        for copy in flat(base_out):
            copy.start()
        base_rcv[k] = base_src[z]

    @pl.when(p == 0)
    def _():
        all_rcv[k] = all_src[0]


    def product(left_re, left_im, right, out):
        @pl.loop(0, SEP // WIDE)
        def _(i):
            cols = pl.ds(pl.multiple_of(i * WIDE, WIDE), WIDE)
            re, im = right[0, :, cols], right[1, :, cols]
            out[0, :, cols] = (dot(left_re, re) - dot(left_im, im)).astype(BF16)
            out[1, :, cols] = (dot(left_re, im) + dot(left_im, re)).astype(BF16)

    def picked(at):
        return (
            dot(selt[at], lv[0, :, :PORT]).astype(BF16),
            dot(selt[at], lv[1, :, :PORT]).astype(BF16),
        )

    @pl.when(p > 0)
    def _():
        left = picked(0)
        product(left[0], left[1], av, aaf)

    @pl.when((p > 0) & (p != CALLER + 1))
    def _():
        aaf_out.start()

    def give_back():
        left = picked(1)
        product(left[0], left[1], av, aab)
        aab_out.start()

    @pl.when((p > CALLER) & (p < last))
    def _():
        give_back()

    for at in range(2):
        for part in range(2):
            lq[at, part] = dot(lv[part, :PORT, :], sel[at]).astype(BF16)

    def resplit():
        @pl.when(first)
        def _():
            pl.semaphore_wait(go_sem, 1)
            piece(2).start()

        @pl.when(jnp.logical_not(first))
        def _():
            pl.semaphore_wait(turn_sem, 1)
            for dz in range(1, SIDE):
                piece(dz).start()

        loads[3].wait()
        for dz in range(1, SIDE):
            piece_in(dz).wait_recv()

        @pl.when(first)
        def _():
            pl.semaphore_signal(turn_sem, inc=1, device_id={"sweep": p - 1}, device_id_type=MESH)

        for part in range(2):
            f2d[part] = f2t[part].T

    @pl.when(p > 0)
    def _():
        resplit()

    loads[2].wait()

    def summed(src, dst, send, recv, step, total):
        for rel in NEAR:
            if step or rel:
                in_copy(src, dst, send, recv, rel, step).wait_recv()
            total = total + dst[origin(rel)].astype(F32)
        return total

    def ask(total, src, dst, out):
        part = cmul(-total, f2d[0], f2d[1]).astype(BF16)
        src[0] = part
        for copy in out:
            copy.start()
        dst[k] = part

    def answer(src, dst, send, recv, old, pieces):
        corr = jnp.zeros((2 * SRC, PORT), F32)
        for dx in reversed(AWAY):
            blk = lax.rem(x + SIDE - dx, SIDE)
            for dz in reversed(AWAY):
                if dx or dz:
                    in_copy(src, dst, send, recv, dx * SIDE + dz, 0).wait_recv()
            parts = [dst[blk * SIDE + row].astype(F32) for row in range(SIDE)]
            if pieces:
                total = jnp.concatenate([part[:, :OWN] for part in parts], axis=1)
            else:
                total = (parts[0] + parts[1]) + (parts[2] + parts[3])
            rows = block_of(blk)
            corr = corr + cmul(total, cv[0, rows, :], cv[1, rows, :])
            f1_s[blk] = f1_s[blk] + total if old else total
        corr_s[...] = corr

    def shifted(blk, plane):
        lane = lax.rem(lax.broadcasted_iota(jnp.int32, blk.shape, 1), PLANES)
        only = jnp.where(lane == plane, blk, 0.0)
        return pltpu.roll(only, (BLK - PLANES + 1) if plane else (PLANES - 1), axis=1)

    def pass_on(na, src, out, plane):
        for dz in AWAY:
            at = lax.rem(z + dz, SIDE)
            cols = block_of(at)
            term = pre_s[at] - cmul(corr_s[...], na[0, :, cols], na[1, :, cols])
            src[at] = term.astype(BF16)
            if dz == 0:
                src[SIDE] = (term - shifted(f1_s[at], plane)).astype(BF16)
            for copy in out[dz]:
                copy.start()

    def edge(at, plane, src, copy):
        src[:, :PORT] = (is_s[...] - cmul(corr_s[...], lq[at, 0], lq[at, 1])).astype(BF16)
        src[:, PORT:] = shifted(f1_s[z], plane).astype(BF16)
        copy.start()

    def prepare(at, inner, aa):
        is_s[...] = dot(inner.astype(BF16), sel[at])
        for blk in range(SIDE):
            cols = slice(blk * BLK, (blk + 1) * BLK)
            pre_s[blk] = cmul(is_s[...], aa[0, :, cols], aa[1, :, cols])

    def corrected(inner):
        return (inner - cmul(corr_s[...], lv[0, :PORT, :], lv[1, :PORT, :])) * live

    zero = jnp.zeros((2 * SRC, BLK), F32)

    def take_edge():
        neighbour(uf_src, uf_rcv, u_send.at[0], u_recv.at[0], -1).wait_recv()

    def take_inner():
        spread = dot(uf_rcv[:, :PORT], selt[0])
        inner_s[...] = inner_s[...] + cmul(spread, lv[0], lv[1])

    @pl.when(p == 0)
    def _():
        total = all_rcv[k].astype(F32)
        for rel in NEAR[1:]:
            in_copy(all_src, all_rcv, base_send, base_recv, rel, 0).wait_recv()
            total = total + all_rcv[origin(rel)].astype(F32)
        let_go()
        whole.wait()
        minus = -total
        part = dot_t(minus.astype(BF16), fo[0]) + dot_t(turned(minus).astype(BF16), fo[1])
        f1_src[0, :, :OWN] = part.astype(BF16)
        for copy in f0_out:
            copy.start()
        f1_rcv[k, :, :OWN] = part.astype(BF16)

    @pl.when((p > 0) & (p != CALLER + 1))
    def _():
        total = summed(base_src, base_rcv, base_send, base_recv, 0, zero)
        total = summed(fwd_src, fwd_rcv, fwd_send, fwd_recv, 1, total)
        ask(total, f1_src, f1_rcv, f1_out)
        take_edge()
        take_inner()

    @pl.when(p == CALLER + 1)
    def _():
        total = summed(base_src, base_rcv, base_send, base_recv, 0, zero)
        take_edge()
        for dz in AWAY:
            at = lax.rem(z + dz, SIDE)
            cols = block_of(at)
            term = cmul(uf_rcv[:, :PORT].astype(F32), aaf[0, :, cols], aaf[1, :, cols])
            own_src[at] = term.astype(BF16)
            for copy in own_out[dz]:
                copy.start()
        fwd_rcv[k] = (own_src[z].astype(F32) - uf_rcv[:, PORT:].astype(F32)).astype(BF16)
        total = summed(own_src, fwd_rcv, own_send, fwd_recv, 0, total)
        ask(total, f1_src, f1_rcv, f1_out)
        take_inner()

    @pl.when(p == CALLER)
    def _():
        is_s[...] = dot(inner_s[...].astype(BF16), sel[1])

    @pl.when((p < last) & (p != CALLER))
    def _():
        neighbour(aaf, aaf_nb, aa_send.at[0], aa_recv.at[0], 1).wait_recv()
        product(lq[1, 0], lq[1, 1], aaf_nb, naf)
        prepare(1, inner_s[...], aaf_nb)

    def take_back():
        neighbour(aab, aab_nb, aa_send.at[1], aa_recv.at[1], -1).wait_recv()
        product(lq[0, 0], lq[0, 1], aab_nb, nab)

    @pl.when(p == last)
    def _():
        take_back()
        prepare(0, inner_s[...], aab_nb)

    @pl.when(p == 0)
    def _():
        answer(*narrow, f1_send, f1_recv, False, True)

    @pl.when(p > 0)
    def _():
        answer(f1_src, f1_rcv, f1_send, f1_recv, False, False)


    @pl.when((p < last) & (p != CALLER))
    def _():
        pass_on(naf, fwd_src, fwd_out, PLANES - 1)

    @pl.when(p < last)
    def _():
        edge(1, PLANES - 1, uf_src, uf_out)

    @pl.when(p == last)
    def _():
        pass_on(nab, bwd_src, bwd_out, 0)
        edge(0, 0, ub_src, ub_out)

    w_s[...] = corrected(inner_s[...])

    @pl.when(p == 0)
    def _():
        resplit()

    @pl.when(p <= CALLER)
    def _():
        give_back()

    @pl.when((p > 0) & (p < last))
    def _():
        take_back()

    @pl.when(p < last)
    def _():
        total = summed(bwd_src, bwd_rcv, bwd_send, bwd_recv, -1, zero)
        ask(total, f2_src, f2_rcv, f2_out)
        neighbour(ub_src, ub_rcv, u_send.at[1], u_recv.at[1], 1).wait_recv()
        spread = dot(ub_rcv[:, :PORT], selt[1])
        innerb_s[...] = cmul(spread, lv[0], lv[1])

    @pl.when((p > 0) & (p < last))
    def _():
        prepare(0, w_s[...] + innerb_s[...], aab_nb)

    @pl.when(p < last)
    def _():
        answer(f2_src, f2_rcv, f2_send, f2_recv, True, False)

    @pl.when((p > 0) & (p < last))
    def _():
        pass_on(nab, bwd_src, bwd_out, 0)
        edge(0, 0, ub_src, ub_out)

    @pl.when(p < last)
    def _():
        w_s[...] = w_s[...] + corrected(innerb_s[...])

    oint_ref[0, 0, 0] = w_s[:SRC, :]
    oint_ref[0, 0, 1] = w_s[SRC:, :]
    block = f1_s[x]
    mine = jnp.zeros((2 * SRC, OWN), F32)
    for owner in range(SIDE):
        mine = jnp.where(z == owner, block[:, owner * OWN : (owner + 1) * OWN], mine)
    osep_ref[0, 0] = mine[:SRC]
    osep_ref[0, 1] = mine[SRC:]

    for dz in range(1, SIDE):
        piece(dz).wait_send()

    @pl.when(p == 0)
    def _():
        for copy in all_out + f0_out:
            copy.wait_send()

    @pl.when(p > 0)
    def _():
        for copy in flat(base_out) + f1_out + flat(bwd_out):
            copy.wait_send()
        ub_out.wait_send()

    @pl.when((p > 0) & (p != CALLER + 1))
    def _():
        aaf_out.wait_send()

    @pl.when(p == CALLER + 1)
    def _():
        for copy in flat(own_out):
            copy.wait_send()

    @pl.when(p < last)
    def _():
        aab_out.wait_send()
        uf_out.wait_send()
        for copy in f2_out:
            copy.wait_send()

    @pl.when((p < last) & (p != CALLER))
    def _():
        for copy in flat(fwd_out):
            copy.wait_send()


def body(rhs_int, rhs_sep, leaf_inv, to_front, to_leaf, front_inv, sizes):
    vmem, anywhere = pl.BlockSpec(memory_space=pltpu.VMEM), pl.BlockSpec(memory_space=pl.ANY)
    rows = 2 * SRC

    def messages(count, width):
        return pltpu.VMEM((count, rows, width), BF16)

    scratch = [
        pltpu.VMEM((2, LEAF, LEAF), BF16),
        pltpu.VMEM((2, PORT, SEP), BF16),
        pltpu.VMEM((2, SEP, PORT), BF16),
        pltpu.VMEM((2, OWN, SEP), BF16),
        pltpu.VMEM((2, BLK, BLK), BF16),
        pltpu.VMEM((2, BLK, BLK), BF16),
        pltpu.VMEM((SIDE, OWN, BLK), BF16),
        pltpu.VMEM((2, LEAF, PORT), BF16),
        pltpu.VMEM((2, PORT, LEAF), BF16),
    ]
    scratch += [pltpu.VMEM((2, PORT, SEP), BF16)] * 6
    scratch += [
        pltpu.VMEM((2, 2, PORT, PORT), BF16),
        pltpu.VMEM((rows, LEAF), F32),
        pltpu.VMEM((rows, LEAF), F32),
        pltpu.VMEM((rows, LEAF), F32),
        pltpu.VMEM((rows, PORT), F32),
        pltpu.VMEM((SIDE, rows, BLK), F32),
        pltpu.VMEM((SIDE, rows, BLK), F32),
        pltpu.VMEM((rows, PORT), F32),
    ]
    scratch += [messages(1, SEP)] + [messages(SIDE + 1, BLK)] * 4 + [messages(1, BLK)] * 2
    scratch += [pltpu.VMEM((rows, PORT + BLK), BF16)] * 2
    scratch += [messages(GROUP, SEP)] + [messages(GROUP, BLK)] * 5 + [pltpu.VMEM((rows, PORT + BLK), BF16)] * 2
    dma = pltpu.SemaphoreType.DMA
    scratch += [pltpu.SemaphoreType.REGULAR] * 2 + [dma((5,)), dma((SIDE,)), dma((SIDE,))] + [dma((2,))] * 4 + [dma((GROUP,))] * 11
    return pl.pallas_call(
        kernel,
        out_shape=(
            jax.ShapeDtypeStruct(rhs_int.shape, F32),
            jax.ShapeDtypeStruct(rhs_sep.shape, F32),
        ),
        in_specs=[vmem, vmem, pl.BlockSpec(memory_space=pltpu.SMEM)] + [anywhere] * 4,
        out_specs=(vmem, vmem),
        scratch_shapes=scratch,
        compiler_params=pltpu.CompilerParams(
            collective_id=0, has_side_effects=True, vmem_limit_bytes=60 << 20
        ),
    )(rhs_int, rhs_sep, sizes, leaf_inv, to_front, to_leaf, front_inv.swapaxes(2, 3))


def solution(mesh):
    placed = (
        P("sweep", "leaf", None, None, None),
        P("sweep", None, None, "leaf"),
        P("sweep", "leaf", None, None, None),
        P("sweep", "leaf", None, None, None),
        P("sweep", "leaf", None, None, None),
        P("sweep", None, None, "leaf"),
        P("sweep", "leaf"),
    )
    return jax.shard_map(
        body,
        mesh=mesh,
        in_specs=placed,
        out_specs=(P("sweep", "leaf", None, None, None), P("sweep", None, None, "leaf")),
        check_vma=False,
    )
```

time: 204 us -> 177 us (0.87)
  Pallas kernels: 195 us -> 173 us
  local copies, waits for them, and re-layouts: 6.67 us -> 2.67 us
    pallas_call x1, Pallas kernels: 195 us -> 173 us  [body(): pl.pallas_call(kernel, out_shape=(jax.ShapeDtypeStruct(rhs_int.shape, F32...]
    unnamed x3 -> x2, local copies, waits for them, and re-layouts: 6.67 us -> 2.67 us
where the time goes in v2:
time: 177 us
  Pallas kernels  173 us (98%)
  local copies, waits for them, and re-layouts  2.67 us (2%)
    pallas_call x1, Pallas kernels, body(): pl.pallas_call(kernel, out_shape=(jax.ShapeDtypeStruct(rhs_int.shape, F32...  173 us

profile of v2, /device:TPU:0, one launch (start us, length us, event | category | flops | bytes accessed | tf_op | source)
XLA Modules:
  0.0 176.6 jit_solution(11740017883438116437)
XLA Ops:
  1.3 172.7 %shard_map.86 = (f32[1,1,2,4,1024]{4,3,2,1,0:T(4,128)}, f32[1,2,4,160]{3,2,1,0:T(4,128)}) custom-call(f32[1,1,2,4,1024]{4,3,2,1,0:T(4,128)} %rint_ref.1, f32[1,2,4,160]{3,2,1,0:T(4,128)} %rsep_ref.1, s32[1,1]{1,0:T(1,128)S(6)} %copy.11.fs_ref, bf16[1,1,2,1024,1024]{4,3,2,1,0:T(8,128)(2,1)} %l_hbm.1, bf16[1,1,2,256,2560]{4,3,2,1,0:T(8,128)(2,1)} %a_hbm.1, ...), custom_call_target="tpu_custom_call" | custom-call | tf_op jit(solution)/shard_map/pallas_call | solution.py:596
  174.0 1.4 copy.12
  175.3 1.3 copy.13

commit v3 on v2

--- a/solution.py
+++ b/solution.py
@@ -49,13 +49,13 @@
 
 
 def kernel(
-    rint_ref, rsep_ref, fs_ref, l_hbm, a_hbm, c_hbm, f_hbm,
+    rint_hbm, rsep_hbm, fs_ref, l_hbm, a_hbm, c_hbm, f_hbm,
     oint_ref, osep_ref,
-    lv, av, cv, fo, f2t, f2d, place, sel, selt, aaf, aab, naf, nab, aaf_nb, aab_nb, lq,
+    rint_ref, rsep_ref, lv, av, cv, fo, f2t, f2d, place, sel, selt, aaf, aab, naf, nab, aaf_nb, aab_nb, lq,
     inner_s, innerb_s, w_s, corr_s, f1_s, pre_s, is_s,
-    all_src, base_src, fwd_src, bwd_src, own_src, f1_src, f2_src, uf_src, ub_src,
-    all_rcv, base_rcv, fwd_rcv, bwd_rcv, f1_rcv, f2_rcv, uf_rcv, ub_rcv,
-    go_sem, turn_sem, load_sem, fp_send, fp_recv, aa_send, aa_recv, u_send, u_recv,
+    base_src, fwd_src, bwd_src, own_src, f1_src, f2_src, uf_src, ub_src, q_rcv,
+    base_rcv, fwd_rcv, bwd_rcv, f1_rcv, f2_rcv, uf_rcv, ub_rcv,
+    go_sem, turn_sem, load_sem, q_send, q_recv, fp_send, fp_recv, aa_send, aa_recv, u_send, u_recv,
     base_send, base_recv, fwd_send, fwd_recv, bwd_send, bwd_recv,
     own_send, f1_send, f1_recv, f2_send, f2_recv,
 ):
@@ -77,21 +77,21 @@
     def owned_by(side):
         return pl.ds(pl.multiple_of(side * OWN, OWN), OWN)
 
-    loads = [
-        pltpu.make_async_copy(l_hbm.at[0, 0], lv, load_sem.at[0]),
-        pltpu.make_async_copy(a_hbm.at[0, 0], av, load_sem.at[1]),
-        pltpu.make_async_copy(c_hbm.at[0, 0], cv, load_sem.at[2]),
+    early = [
+        pltpu.make_async_copy(rint_hbm.at[0, 0], rint_ref, load_sem.at[0]),
+        pltpu.make_async_copy(l_hbm.at[0, 0], lv, load_sem.at[1]),
+        pltpu.make_async_copy(rsep_hbm.at[0], rsep_ref, load_sem.at[2]),
+        pltpu.make_async_copy(a_hbm.at[0, 0], av, load_sem.at[3]),
+    ]
+    late = [
+        pltpu.make_async_copy(c_hbm.at[0, 0], cv, load_sem.at[4]),
         pltpu.make_async_copy(
-            f_hbm.at[0, :, :, block_of(z)], f2t.at[:, owned_by(z), :], load_sem.at[3]
+            f_hbm.at[0, :, :, block_of(z)], f2t.at[:, owned_by(z), :], load_sem.at[5]
         ),
     ]
-    for load in loads:
+    whole = pltpu.make_async_copy(f_hbm.at[0], fo, load_sem.at[6])
+    for load in early:
         load.start()
-    whole = pltpu.make_async_copy(f_hbm.at[0], fo, load_sem.at[4])
-
-    @pl.when(p == 0)
-    def _():
-        whole.start()
 
     barrier = pltpu.get_barrier_semaphore()
     for rel in range(1, GROUP):
@@ -126,6 +126,23 @@
             == lax.broadcasted_iota(jnp.int32, (OWN, BLK), 0) + k * OWN
         )
         place[blk] = jnp.where(hit, 1.0, 0.0).astype(BF16)
+
+    col = lax.broadcasted_iota(jnp.int32, (1, LEAF), 1)
+    live = jnp.where(col < size, 1.0, 0.0).astype(F32)
+
+    def rows_of(ref):
+        return jnp.concatenate([ref[0], ref[1]], axis=0)
+
+    early[0].wait()
+    early[1].wait()
+    inner_s[...] = cmul(rows_of(rint_ref) * live, lv[0], lv[1])
+    early[2].wait()
+    early[3].wait()
+    own = rows_of(rsep_ref).astype(BF16)
+    for blk in range(SIDE):
+        cols = slice(blk * BLK, (blk + 1) * BLK)
+        term = cmul(inner_s[:, :PORT], av[0, :, cols], av[1, :, cols]) - dot(own, place[blk])
+        base_src[blk] = term.astype(BF16)
 
     @pl.when((p > 0) & (p < last))
     def _():
@@ -207,9 +224,17 @@
     narrow = f1_src.at[:, :, :PORT], f1_rcv.at[:, :, :PORT]
 
     base_out = term_sends(base_src, base_rcv, base_send, base_recv, 0)
-    all_out = f_sends(all_src, all_rcv, base_send, base_recv)
     own_out = term_sends(own_src, fwd_rcv, own_send, fwd_recv, 0)
     f0_out = f_sends(*narrow, f1_send, f1_recv)
+
+    def ring(dz, sign):
+        there = lax.rem(z + SIDE + sign * dz, SIDE)
+        slot = z if sign > 0 else there
+        return pltpu.make_async_remote_copy(
+            q_rcv.at[slot], q_rcv.at[slot], q_send.at[dz], q_recv.at[dz],
+            device_id={"leaf": x * SIDE + there}, device_id_type=MESH,
+        )
+
     fwd_out = term_sends(fwd_src, fwd_rcv, fwd_send, fwd_recv, 1)
     bwd_out = term_sends(bwd_src, bwd_rcv, bwd_send, bwd_recv, -1)
     f1_out = f_sends(f1_src, f1_rcv, f1_send, f1_recv)
@@ -228,37 +253,16 @@
     uf_out = neighbour(uf_src, uf_rcv, u_send.at[0], u_recv.at[0], 1)
     ub_out = neighbour(ub_src, ub_rcv, u_send.at[1], u_recv.at[1], -1)
 
-    col = lax.broadcasted_iota(jnp.int32, (1, LEAF), 1)
-    live = jnp.where(col < size, 1.0, 0.0).astype(F32)
-
-    def rows_of(ref):
-        return jnp.concatenate([ref[0], ref[1]], axis=0)
-
-    loads[0].wait()
-    inner_s[...] = cmul(rows_of(rint_ref[0, 0]) * live, lv[0], lv[1])
-    loads[1].wait()
-    own = rows_of(rsep_ref[0]).astype(BF16)
-    for blk in range(SIDE):
-        cols = slice(blk * BLK, (blk + 1) * BLK)
-        term = cmul(inner_s[:, :PORT], av[0, :, cols], av[1, :, cols]) - dot(own, place[blk])
-        base_src[blk] = term.astype(BF16)
-        all_src[0, :, cols] = term.astype(BF16)
+    for copy in late:
+        copy.start()
 
     @pl.when(p == 0)
     def _():
-        for copy in all_out:
-            copy.start()
-
-    @pl.when(p > 0)
-    def _():
-        for copy in flat(base_out):
-            copy.start()
-        base_rcv[k] = base_src[z]
-
-    @pl.when(p == 0)
-    def _():
-        all_rcv[k] = all_src[0]
-
+        whole.start()
+
+    for copy in flat(base_out):
+        copy.start()
+    base_rcv[k] = base_src[z]
 
     def product(left_re, left_im, right, out):
         @pl.loop(0, SEP // WIDE)
@@ -300,7 +304,8 @@
         @pl.when(first)
         def _():
             pl.semaphore_wait(go_sem, 1)
-            piece(2).start()
+            for dz in (2,):
+                piece(dz).start()
 
         @pl.when(jnp.logical_not(first))
         def _():
@@ -308,7 +313,7 @@
             for dz in range(1, SIDE):
                 piece(dz).start()
 
-        loads[3].wait()
+        late[1].wait()
         for dz in range(1, SIDE):
             piece_in(dz).wait_recv()
 
@@ -323,7 +328,7 @@
     def _():
         resplit()
 
-    loads[2].wait()
+    late[0].wait()
 
     def summed(src, dst, send, recv, step, total):
         for rel in NEAR:
@@ -362,10 +367,12 @@
         return pltpu.roll(only, (BLK - PLANES + 1) if plane else (PLANES - 1), axis=1)
 
     def pass_on(na, src, out, plane):
+        corr = corr_s[...]
+        corr_re, corr_im = corr.astype(BF16), turned(corr).astype(BF16)
         for dz in AWAY:
             at = lax.rem(z + dz, SIDE)
             cols = block_of(at)
-            term = pre_s[at] - cmul(corr_s[...], na[0, :, cols], na[1, :, cols])
+            term = pre_s[at] - (dot(corr_re, na[0, :, cols]) + dot(corr_im, na[1, :, cols]))
             src[at] = term.astype(BF16)
             if dz == 0:
                 src[SIDE] = (term - shifted(f1_s[at], plane)).astype(BF16)
@@ -397,14 +404,16 @@
 
     @pl.when(p == 0)
     def _():
-        total = all_rcv[k].astype(F32)
-        for rel in NEAR[1:]:
-            in_copy(all_src, all_rcv, base_send, base_recv, rel, 0).wait_recv()
-            total = total + all_rcv[origin(rel)].astype(F32)
+        total = summed(base_src, base_rcv, base_send, base_recv, 0, zero)
         let_go()
+        q_rcv[z] = (-total).astype(BF16)
+        for dz in AWAY[:-1]:
+            ring(dz, 1).start()
+        for dz in AWAY[:-1]:
+            ring(dz, -1).wait_recv()
         whole.wait()
-        minus = -total
-        part = dot_t(minus.astype(BF16), fo[0]) + dot_t(turned(minus).astype(BF16), fo[1])
+        full = jnp.concatenate([q_rcv[at].astype(F32) for at in range(SIDE)], axis=1)
+        part = dot_t(full.astype(BF16), fo[0]) + dot_t(turned(full).astype(BF16), fo[1])
         f1_src[0, :, :OWN] = part.astype(BF16)
         for copy in f0_out:
             copy.start()
@@ -528,8 +537,10 @@
 
     @pl.when(p == 0)
     def _():
-        for copy in all_out + f0_out:
+        for copy in flat(base_out) + f0_out:
             copy.wait_send()
+        for dz in AWAY[:-1]:
+            ring(dz, 1).wait_send()
 
     @pl.when(p > 0)
     def _():
@@ -560,13 +571,15 @@
 
 
 def body(rhs_int, rhs_sep, leaf_inv, to_front, to_leaf, front_inv, sizes):
-    vmem, anywhere = pl.BlockSpec(memory_space=pltpu.VMEM), pl.BlockSpec(memory_space=pl.ANY)
+    vmem, hbm = pl.BlockSpec(memory_space=pltpu.VMEM), pl.BlockSpec(memory_space=pltpu.HBM)
     rows = 2 * SRC
 
     def messages(count, width):
         return pltpu.VMEM((count, rows, width), BF16)
 
     scratch = [
+        pltpu.VMEM((2, SRC, LEAF), F32),
+        pltpu.VMEM((2, SRC, OWN), F32),
         pltpu.VMEM((2, LEAF, LEAF), BF16),
         pltpu.VMEM((2, PORT, SEP), BF16),
         pltpu.VMEM((2, SEP, PORT), BF16),
@@ -588,22 +601,22 @@
         pltpu.VMEM((SIDE, rows, BLK), F32),
         pltpu.VMEM((rows, PORT), F32),
     ]
-    scratch += [messages(1, SEP)] + [messages(SIDE + 1, BLK)] * 4 + [messages(1, BLK)] * 2
+    scratch += [messages(SIDE + 1, BLK)] * 4 + [messages(1, BLK)] * 2
     scratch += [pltpu.VMEM((rows, PORT + BLK), BF16)] * 2
-    scratch += [messages(GROUP, SEP)] + [messages(GROUP, BLK)] * 5 + [pltpu.VMEM((rows, PORT + BLK), BF16)] * 2
+    scratch += [messages(SIDE, BLK)] + [messages(GROUP, BLK)] * 5 + [pltpu.VMEM((rows, PORT + BLK), BF16)] * 2
     dma = pltpu.SemaphoreType.DMA
-    scratch += [pltpu.SemaphoreType.REGULAR] * 2 + [dma((5,)), dma((SIDE,)), dma((SIDE,))] + [dma((2,))] * 4 + [dma((GROUP,))] * 11
+    scratch += [pltpu.SemaphoreType.REGULAR] * 2 + [dma((7,))] + [dma((SIDE,))] * 4 + [dma((2,))] * 4 + [dma((GROUP,))] * 11
     return pl.pallas_call(
         kernel,
         out_shape=(
             jax.ShapeDtypeStruct(rhs_int.shape, F32),
             jax.ShapeDtypeStruct(rhs_sep.shape, F32),
         ),
-        in_specs=[vmem, vmem, pl.BlockSpec(memory_space=pltpu.SMEM)] + [anywhere] * 4,
+        in_specs=[hbm, hbm, pl.BlockSpec(memory_space=pltpu.SMEM)] + [hbm] * 4,
         out_specs=(vmem, vmem),
         scratch_shapes=scratch,
         compiler_params=pltpu.CompilerParams(
-            collective_id=0, has_side_effects=True, vmem_limit_bytes=60 << 20
+            collective_id=0, has_side_effects=True, vmem_limit_bytes=53 << 20
         ),
     )(rhs_int, rhs_sep, sizes, leaf_inv, to_front, to_leaf, front_inv.swapaxes(2, 3))
 

time: 177 us -> 175 us (0.989)
  Pallas kernels: 173 us -> 171 us
    pallas_call x1, Pallas kernels: 173 us -> 171 us  [body(): pl.pallas_call(kernel, out_shape=(jax.ShapeDtypeStruct(rhs_int.shape, F32...]
where the time goes in v3:
time: 175 us
  Pallas kernels  171 us (98%)
  local copies, waits for them, and re-layouts  2.66 us (2%)
    pallas_call x1, Pallas kernels, body(): pl.pallas_call(kernel, out_shape=(jax.ShapeDtypeStruct(rhs_int.shape, F32...  171 us

profile of v3, /device:TPU:0, one launch (start us, length us, event | category | flops | bytes accessed | tf_op | source)
XLA Modules:
  0.0 174.7 jit_solution(13573675329181552343)
XLA Ops:
  1.3 0.0 copy-start
  1.3 0.7 copy-done
  2.0 0.0 copy-start.1
  2.0 0.7 copy-done.1
  2.7 170.8 %shard_map.86 = (f32[1,1,2,4,1024]{4,3,2,1,0:T(4,128)S(1)}, f32[1,2,4,160]{3,2,1,0:T(4,128)S(1)}) custom-call(f32[1,1,2,4,1024]{4,3,2,1,0:T(4,128)S(1)} %copy-done, f32[1,2,4,160]{3,2,1,0:T(4,128)S(1)} %copy-done.1, s32[1,1]{1,0:T(1,128)S(6)} %copy.11.fs_ref, bf16[1,1,2,1024,1024]{4,3,2,1,0:T(8,128)(2,1)} %l_hbm.1, bf16[1,1,2,256,2560]{4,3,2,1,0:T(8,128)(2,1)} %a_hbm.1, ...), custom_call_target="tpu_custom_call" | custom-call | tf_op jit(solution)/shard_map/pallas_call | solution.py:609
  173.5 0.6 copy.12
  174.1 0.6 copy.13
Async XLA Ops:
  1.3 0.8 copy-start
  2.0 0.7 copy-start.1

commit v4 on v3

--- a/solution.py
+++ b/solution.py
@@ -317,7 +317,7 @@
         for dz in range(1, SIDE):
             piece_in(dz).wait_recv()
 
-        @pl.when(first)
+        @pl.when(first & (p != CALLER))
         def _():
             pl.semaphore_signal(turn_sem, inc=1, device_id={"sweep": p - 1}, device_id_type=MESH)
 
@@ -483,6 +483,10 @@
     def _():
         pass_on(nab, bwd_src, bwd_out, 0)
         edge(0, 0, ub_src, ub_out)
+
+    @pl.when(p == CALLER)
+    def _():
+        pl.semaphore_signal(turn_sem, inc=1, device_id={"sweep": p - 1}, device_id_type=MESH)
 
     w_s[...] = corrected(inner_s[...])
 

time: 175 us -> 174 us (level)
  no operation moved by 1% of the time
where the time goes in v4:
time: 174 us
  Pallas kernels  170 us (98%)
  local copies, waits for them, and re-layouts  2.66 us (2%)
    pallas_call x1, Pallas kernels, body(): pl.pallas_call(kernel, out_shape=(jax.ShapeDtypeStruct(rhs_int.shape, F32...  170 us

profile of v4, /device:TPU:0, one launch (start us, length us, event | category | flops | bytes accessed | tf_op | source)
XLA Modules:
  0.0 173.8 jit_solution(5406830305807617123)
XLA Ops:
  1.3 0.0 copy-start
  1.3 0.7 copy-done
  2.0 0.0 copy-start.1
  2.0 0.7 copy-done.1
  2.7 169.8 %shard_map.86 = (f32[1,1,2,4,1024]{4,3,2,1,0:T(4,128)S(1)}, f32[1,2,4,160]{3,2,1,0:T(4,128)S(1)}) custom-call(f32[1,1,2,4,1024]{4,3,2,1,0:T(4,128)S(1)} %copy-done, f32[1,2,4,160]{3,2,1,0:T(4,128)S(1)} %copy-done.1, s32[1,1]{1,0:T(1,128)S(6)} %copy.11.fs_ref, bf16[1,1,2,1024,1024]{4,3,2,1,0:T(8,128)(2,1)} %l_hbm.1, bf16[1,1,2,256,2560]{4,3,2,1,0:T(8,128)(2,1)} %a_hbm.1, ...), custom_call_target="tpu_custom_call" | custom-call | tf_op jit(solution)/shard_map/pallas_call | solution.py:613
  172.6 0.6 copy.12
  173.2 0.6 copy.13
Async XLA Ops:
  1.3 0.8 copy-start
  2.0 0.7 copy-start.1
